TPU v7x, 32 devices: a whole 2x2x4 slice. The times are simulated.
32 devices in a mesh: ep: 16 (over z, x, core), hs: 2 (over y).
Axes of the slice: x: 2, y: 2, z: 4, core: 2. Of those that a mesh axis runs over, the one named last changes fastest.
Arguments:
- tokens: bfloat16 [8192, 1024], P(('ep', 'hs')), may hold values from -6 to 6
- segment_ids: int32 [32, 256], P(('ep', 'hs')), may hold values from 0 to 3, never falling along the last dimension, each value on 1 to 128 neighbouring positions
- live_mask: int32 [32, 256], P(('ep', 'hs')), may hold values 0 or 1
- routes: int32 [8192, 8], P(('ep', 'hs')), may hold values from 0 to 15, all different within a row; in each aligned block of 256 rows (0 to 255, 256 to 511, ...) at most 256 rows name the same one
- attn_gain: float32 [1024], replicated, may hold values from 0.25 to 1.75
- w_query: bfloat16 [1024, 1024], replicated, may hold values from -0.1875 to 0.1875
- key_weight: bfloat16 [1024, 512], replicated, may hold values from -0.1875 to 0.1875
- value_weight: bfloat16 [1024, 512], replicated, may hold values from -0.1875 to 0.1875
- w_out: bfloat16 [1024, 1024], replicated, may hold values from -1 to 1
- moe_gain: float32 [1024], replicated, may hold values from 0.25 to 1.75
- router: bfloat16 [1024, 16], replicated, may hold values from -0.09375 to 0.09375
- w_gate: bfloat16 [16, 1024, 512], P('ep', None, 'hs'), may hold values from -0.1875 to 0.1875
- w_up: bfloat16 [16, 1024, 512], P('ep', None, 'hs'), may hold values from -0.1875 to 0.1875
- w_down: bfloat16 [16, 512, 1024], P('ep', 'hs'), may hold values from -0.75 to 0.75
- cotangent: bfloat16 [8192, 1024], P(('ep', 'hs')), may hold values from -6 to 6
Outputs:
- output: bfloat16 [8192, 1024], P(('ep', 'hs'))
- input_grad: float32 [8192, 1024], P(('ep', 'hs'))
- attn_gain_grad: float32 [1024], replicated
- query_grad: float32 [1024, 1024], replicated
- key_grad: float32 [1024, 512], replicated
- value_grad: float32 [1024, 512], replicated
- out_grad: float32 [1024, 1024], replicated
- moe_gain_grad: float32 [1024], replicated
- router_grad: float32 [1024, 16], replicated
- gate_grad: float32 [16, 1024, 512], P('ep', None, 'hs')
- up_grad: float32 [16, 1024, 512], P('ep', None, 'hs')
- down_grad: float32 [16, 512, 1024], P('ep', 'hs')
- expert_counts: int32 [16], replicated
Inputs may be any that keep to these rules, and one draw needn't show every extreme that they name: `segment_ids`: document numbers never fall along a row; a document has at most 128 tokens, and one has exactly that many. `routes`: each token names 8 different experts. The 256 tokens of one row name one expert at most 256 times, a bound that some block reaches.
All inputs are finite; a program needn't handle non-finite values. No bound on the sum of `live_mask` on one device may be relied on, other than what follows from the above.
Results may differ from a plain program's by a relative error of at most 0.013.
The roundings to bfloat16 on the way count: a program that leaves them out, or rounds other values in their place, can miss the bound.
Values may be sent and summed in bfloat16 or wider, within the bound.
A program may use at most 384 MiB of HBM per device.

v0:
```python
import jax
import jax.numpy as jnp
from jax import lax
from jax.sharding import PartitionSpec as P

QUERY_HEADS = 16
KEY_VALUE_HEADS = 8
HEAD_SIZE = 64
TOP = 8
EPSILON = 1e-05


def rms_forward(value_rows, norm_gain):
    inverse = lax.rsqrt(jnp.mean(value_rows * value_rows, axis=-1, keepdims=True) + EPSILON)
    return (value_rows * inverse * norm_gain, inverse)


def rms_backward(value_rows, inverse, norm_gain, upstream):
    scaled = upstream * norm_gain
    gain_grad = jnp.sum(upstream * value_rows * inverse, axis=0)
    input_grad = inverse * (
        scaled
        - value_rows * inverse * inverse * jnp.mean(scaled * value_rows, axis=-1, keepdims=True)
    )
    return (input_grad, gain_grad)


def positions_of(segment):
    before = (segment[None, :] < segment[:, None]).astype(jnp.int32)
    return jnp.arange(segment.shape[-1], dtype=jnp.int32) - jnp.sum(before, axis=1)


def rotary_tables(positions, head_dim):
    half_dim = head_dim // 2
    frequency = 10000.0 ** (-(jnp.arange(half_dim, dtype=jnp.float32) * 2.0) / head_dim)
    angles = positions.astype(jnp.float32)[:, None] * frequency[None, :]
    return (jnp.cos(angles)[:, None, :], jnp.sin(angles)[:, None, :])


def rotary(heads, cosine_table, sine_table):
    half_dim = heads.shape[-1] // 2
    first_half = heads[..., :half_dim]
    second_half = heads[..., half_dim:]
    return jnp.concatenate(
        [
            first_half * cosine_table - second_half * sine_table,
            second_half * cosine_table + first_half * sine_table,
        ],
        axis=-1,
    )


def rotary_backward(grads, cosine_table, sine_table):
    half_dim = grads.shape[-1] // 2
    first_half = grads[..., :half_dim]
    second_half = grads[..., half_dim:]
    return jnp.concatenate(
        [
            first_half * cosine_table + second_half * sine_table,
            second_half * cosine_table - first_half * sine_table,
        ],
        axis=-1,
    )


def to_bf16(value):
    return lax.reduce_precision(value, 8, 7)


def expert_pass(rows, upstream, gates, gate_w, up_w, down_w):
    groups, model_dim, width = gate_w.shape
    gate_all = jnp.concatenate([gate_w[j] for j in range(groups)], axis=1)
    up_all = jnp.concatenate([up_w[j] for j in range(groups)], axis=1)
    down_all = down_w.reshape(groups * width, model_dim)
    gate_pre = jnp.dot(rows, gate_all, preferred_element_type=jnp.float32)
    up_pre = jnp.dot(rows, up_all, preferred_element_type=jnp.float32)
    sigmoid_part = jax.nn.sigmoid(gate_pre)
    activated = gate_pre * sigmoid_part
    hidden = (activated * up_pre).astype(jnp.bfloat16)
    total = jnp.zeros(rows.shape, jnp.float32)
    for j in range(groups):
        total = total + to_bf16(
            jnp.dot(
                hidden[:, j * width : (j + 1) * width],
                down_w[j],
                preferred_element_type=jnp.float32,
            )
        )
    total = to_bf16(total)
    upstream_f = upstream.astype(jnp.float32)
    gate_upstream = jnp.sum(upstream_f * total, axis=-1)
    weighted = (gates[:, None] * total).astype(jnp.bfloat16)
    upstream_e = (gates[:, None] * upstream_f).astype(jnp.bfloat16)
    hidden_grad = jnp.einsum("td,fd->tf", upstream_e, down_all, preferred_element_type=jnp.float32)
    up_pre_grad = (hidden_grad * activated).astype(jnp.bfloat16)
    gate_pre_grad = (
        hidden_grad * up_pre * sigmoid_part * (1.0 + gate_pre * (1.0 - sigmoid_part))
    ).astype(jnp.bfloat16)
    down_grad = jnp.einsum("tf,td->fd", hidden, upstream_e, preferred_element_type=jnp.float32)
    gate_grad = jnp.einsum("td,tf->df", rows, gate_pre_grad, preferred_element_type=jnp.float32)
    up_grad = jnp.einsum("td,tf->df", rows, up_pre_grad, preferred_element_type=jnp.float32)
    back = jnp.zeros(rows.shape, jnp.float32)
    for j in range(groups):
        cut = slice(j * width, (j + 1) * width)
        back = back + to_bf16(
            jnp.einsum(
                "tf,df->td", gate_pre_grad[:, cut], gate_w[j], preferred_element_type=jnp.float32
            )
            + jnp.einsum(
                "tf,df->td", up_pre_grad[:, cut], up_w[j], preferred_element_type=jnp.float32
            )
        )
    return (weighted, back.astype(jnp.bfloat16), gate_upstream, gate_grad, up_grad, down_grad)


def local(
    tokens,
    segment_ids,
    live_mask,
    routes,
    attn_gain,
    w_query,
    key_weight,
    value_weight,
    w_out,
    moe_gain,
    router,
    w_gate,
    w_up,
    w_down,
    cotangent,
):
    sequence_length = tokens.shape[0]
    model_dim = tokens.shape[1]
    experts_all = router.shape[1]
    query_per_key_head = QUERY_HEADS // KEY_VALUE_HEADS
    score_scale = HEAD_SIZE ** (-0.5)
    upstream_all = lax.all_gather(cotangent, "ep", axis=0, tiled=True)
    gate_all = lax.all_gather(w_gate, "hs", axis=0, tiled=True)
    up_all = lax.all_gather(w_up, "hs", axis=0, tiled=True)
    down_all = lax.all_gather(w_down, "hs", axis=0, tiled=True)
    segment = segment_ids[0]
    live_row = live_mask[0]
    inputs = tokens.astype(jnp.float32)
    normed_rows, inverse_one = rms_forward(inputs, attn_gain)
    normed_rows_back = normed_rows.astype(jnp.bfloat16)
    query_pre = jnp.dot(normed_rows_back, w_query, preferred_element_type=jnp.float32).reshape(
        sequence_length, QUERY_HEADS, HEAD_SIZE
    )
    key_before_rotary = jnp.dot(
        normed_rows_back, key_weight, preferred_element_type=jnp.float32
    ).reshape(sequence_length, KEY_VALUE_HEADS, HEAD_SIZE)
    value_b = (
        jnp.dot(normed_rows_back, value_weight, preferred_element_type=jnp.float32)
        .astype(jnp.bfloat16)
        .reshape(sequence_length, KEY_VALUE_HEADS, HEAD_SIZE)
    )
    positions = positions_of(segment)
    cosine_table, sine_table = rotary_tables(positions, HEAD_SIZE)
    query_back_rows = rotary(query_pre, cosine_table, sine_table).astype(jnp.bfloat16)
    key_b = rotary(key_before_rotary, cosine_table, sine_table).astype(jnp.bfloat16)
    indices = jnp.arange(sequence_length)
    allowed = (
        (segment[:, None] == segment[None, :])
        & (indices[None, :] <= indices[:, None])
        & ((live_row[None, :] > 0) | (indices[None, :] == indices[:, None]))
    )
    grouped_rows = query_back_rows.reshape(
        sequence_length, KEY_VALUE_HEADS, query_per_key_head, HEAD_SIZE
    )
    scores = (
        jnp.einsum("qgrd,kgd->grqk", grouped_rows, key_b, preferred_element_type=jnp.float32)
        * score_scale
    )
    scores = jnp.where(allowed, scores, -1e30)
    highest = jnp.max(scores, axis=-1, keepdims=True)
    weights_exp = jnp.exp(scores - highest)
    denominator = jnp.sum(weights_exp, axis=-1, keepdims=True)
    log_total = highest + jnp.log(denominator)
    probabilities = weights_exp / denominator
    mixed = jnp.einsum(
        "grqk,kgd->qgrd",
        probabilities.astype(jnp.bfloat16),
        value_b,
        preferred_element_type=jnp.float32,
    )
    mixed_b = mixed.reshape(sequence_length, QUERY_HEADS * HEAD_SIZE).astype(jnp.bfloat16)
    middle = inputs + jnp.dot(mixed_b, w_out, preferred_element_type=jnp.float32)
    moe_normed, inverse_two = rms_forward(middle, moe_gain)
    moe_in = moe_normed.astype(jnp.bfloat16)
    logits = jnp.dot(moe_in, router, preferred_element_type=jnp.float32)
    route_hot = (routes[:, :, None] == jnp.arange(experts_all)[None, None, :]).astype(jnp.float32)
    chosen = jnp.sum(route_hot * logits[:, None, :], axis=-1)
    route_soft = jax.nn.softmax(chosen, axis=-1)
    live_column = live_row.astype(jnp.float32)[:, None]
    route_gates = route_soft * live_column
    counts_local = jnp.sum(route_hot * live_column[:, :, None], axis=(0, 1))
    dense_gates = jnp.sum(route_hot * route_gates[:, :, None], axis=1)
    rows_all = lax.all_gather(moe_in, "ep", axis=0, tiled=True)
    gates_all = lax.all_to_all(
        dense_gates.T.reshape(experts_all, 1, sequence_length),
        "ep",
        split_axis=0,
        concat_axis=1,
        tiled=True,
    ).reshape(-1)
    weighted, back, gate_upstream_all, gate_w_grad, up_w_grad, down_w_grad = expert_pass(
        rows_all, upstream_all, gates_all, gate_all, up_all, down_all
    )
    combined = lax.psum_scatter(weighted, "ep", scatter_dimension=0, tiled=True).astype(jnp.float32)
    expert_input_grad = lax.psum_scatter(back, "ep", scatter_dimension=0, tiled=True).astype(
        jnp.float32
    )
    output = (middle + combined).astype(jnp.bfloat16)
    upstream = cotangent.astype(jnp.float32)
    gate_upstream_dense = (
        lax.all_to_all(
            gate_upstream_all.reshape(experts_all, 1, sequence_length),
            "ep",
            split_axis=0,
            concat_axis=1,
            tiled=True,
        )
        .reshape(experts_all, sequence_length)
        .T
    )
    gate_upstream = jnp.sum(route_hot * gate_upstream_dense[:, None, :], axis=-1)
    gate_w_grad = lax.psum_scatter(gate_w_grad, "hs", scatter_dimension=1, tiled=True)[None]
    up_w_grad = lax.psum_scatter(up_w_grad, "hs", scatter_dimension=1, tiled=True)[None]
    down_w_grad = lax.psum_scatter(down_w_grad, "hs", scatter_dimension=0, tiled=True)[None]
    soft_upstream = gate_upstream * live_column
    chosen_grad = route_soft * (
        soft_upstream - jnp.sum(route_soft * soft_upstream, axis=-1, keepdims=True)
    )
    logit_grad = jnp.sum(route_hot * chosen_grad[:, :, None], axis=1).astype(jnp.bfloat16)
    router_w_grad = jnp.einsum("td,te->de", moe_in, logit_grad, preferred_element_type=jnp.float32)
    moe_in_grad = expert_input_grad + jnp.einsum(
        "te,de->td", logit_grad, router, preferred_element_type=jnp.float32
    )
    middle_norm_grad, moe_gain_grad = rms_backward(middle, inverse_two, moe_gain, moe_in_grad)
    middle_grad = upstream + middle_norm_grad
    attn_grad_b = middle_grad.astype(jnp.bfloat16)
    out_w_grad = jnp.einsum("tm,td->md", mixed_b, attn_grad_b, preferred_element_type=jnp.float32)
    attention_mixed_grad = jnp.einsum(
        "td,md->tm", attn_grad_b, w_out, preferred_element_type=jnp.float32
    ).astype(jnp.bfloat16)
    attention_mixed_grad = attention_mixed_grad.reshape(
        sequence_length, KEY_VALUE_HEADS, query_per_key_head, HEAD_SIZE
    )
    scores_again = (
        jnp.einsum("qgrd,kgd->grqk", grouped_rows, key_b, preferred_element_type=jnp.float32)
        * score_scale
    )
    scores_again = jnp.where(allowed, scores_again, -1e30)
    probs_again = jnp.exp(scores_again - log_total)
    prob_grad = jnp.einsum(
        "qgrd,kgd->grqk", attention_mixed_grad, value_b, preferred_element_type=jnp.float32
    )
    value_per_head_grad = jnp.einsum(
        "grqk,qgrd->kgd",
        probs_again.astype(jnp.bfloat16),
        attention_mixed_grad,
        preferred_element_type=jnp.float32,
    )
    value_per_head_grad = value_per_head_grad.astype(jnp.bfloat16).reshape(
        sequence_length, KEY_VALUE_HEADS * HEAD_SIZE
    )
    row_delta = jnp.sum(probs_again * prob_grad, axis=-1, keepdims=True)
    score_grad = (probs_again * (prob_grad - row_delta)).astype(jnp.bfloat16)
    query_rot_grad = (
        jnp.einsum("grqk,kgd->qgrd", score_grad, key_b, preferred_element_type=jnp.float32)
        * score_scale
    )
    rotated_key_grad = (
        jnp.einsum("grqk,qgrd->kgd", score_grad, grouped_rows, preferred_element_type=jnp.float32)
        * score_scale
    )
    query_head_grad = (
        rotary_backward(
            query_rot_grad.reshape(sequence_length, QUERY_HEADS, HEAD_SIZE),
            cosine_table,
            sine_table,
        )
        .astype(jnp.bfloat16)
        .reshape(sequence_length, QUERY_HEADS * HEAD_SIZE)
    )
    key_head_grad = (
        rotary_backward(rotated_key_grad, cosine_table, sine_table)
        .astype(jnp.bfloat16)
        .reshape(sequence_length, KEY_VALUE_HEADS * HEAD_SIZE)
    )
    query_w_grad = jnp.einsum(
        "td,te->de", normed_rows_back, query_head_grad, preferred_element_type=jnp.float32
    )
    key_w_grad = jnp.einsum(
        "td,te->de", normed_rows_back, key_head_grad, preferred_element_type=jnp.float32
    )
    value_w_grad = jnp.einsum(
        "td,te->de", normed_rows_back, value_per_head_grad, preferred_element_type=jnp.float32
    )
    normed_grad = jnp.einsum(
        "te,de->td", query_head_grad, w_query, preferred_element_type=jnp.float32
    )
    normed_grad = normed_grad + jnp.einsum(
        "te,de->td", key_head_grad, key_weight, preferred_element_type=jnp.float32
    )
    normed_grad = normed_grad + jnp.einsum(
        "te,de->td", value_per_head_grad, value_weight, preferred_element_type=jnp.float32
    )
    input_norm_grad, attn_gain_grad = rms_backward(inputs, inverse_one, attn_gain, normed_grad)
    input_grad = middle_grad + input_norm_grad
    shared = lax.psum(
        (
            attn_gain_grad,
            query_w_grad,
            key_w_grad,
            value_w_grad,
            out_w_grad,
            moe_gain_grad,
            router_w_grad,
            counts_local,
        ),
        ("ep", "hs"),
    )
    return (
        output,
        input_grad,
        shared[0],
        shared[1],
        shared[2],
        shared[3],
        shared[4],
        shared[5],
        shared[6],
        gate_w_grad,
        up_w_grad,
        down_w_grad,
        shared[7].astype(jnp.int32),
    )


def solution(mesh):
    in_specs = (
        P(("ep", "hs"), None),
        P(("ep", "hs"), None),
        P(("ep", "hs"), None),
        P(("ep", "hs"), None),
        P(),
        P(),
        P(),
        P(),
        P(),
        P(),
        P(),
        P("ep", None, "hs"),
        P("ep", None, "hs"),
        P("ep", "hs", None),
        P(("ep", "hs"), None),
    )
    out_specs = (
        P(("ep", "hs"), None),
        P(("ep", "hs"), None),
        P(),
        P(),
        P(),
        P(),
        P(),
        P(),
        P(),
        P("ep", None, "hs"),
        P("ep", None, "hs"),
        P("ep", "hs", None),
        P(),
    )
    return jax.shard_map(local, mesh=mesh, in_specs=in_specs, out_specs=out_specs, check_vma=False)
```

profile of v0, /device:TPU:0, one launch (start us, length us, event | category | flops | bytes accessed | tf_op | source)
XLA Modules:
  0.0 911.5 jit_solution(5875552281925861520)
XLA Ops:
  27.0 6.6 all-gather.10.cloned.1.call-done
  34.9 21.6 %all-gather.8.cloned.1.call-done = bf16[2,1024,256]{2,1,0:T(8,128)(2,1)} async-done(((bf16[1,1024,256]{2,1,0:T(8,128)(2,1)}), bf16[2,1024,256]{2,1,0:T(8,128)(2,1)}) %all-gather.8.cloned.1.call-update) | async-done | bytes 1048592 | tf_op jit(solution)/shard_map/all_gather | solution.py:139
  58.8 75.4 %all-gather.6.cloned.1.call-done = bf16[4096,1024]{1,0:T(8,128)(2,1)} async-done(((bf16[256,1024]{1,0:T(8,128)(2,1)}), bf16[4096,1024]{1,0:T(8,128)(2,1)}) %all-gather.6.cloned.1.call-update) | async-done | bytes 8388624 | tf_op jit(solution)/shard_map/all_gather | solution.py:199
  134.2 8.0 fusion.46
  145.4 8.8 multiply_convert_fusion.3
  155.2 9.9 %fusion.22 = f32[4096,1024]{1,0:T(8,128)} fusion(bf16[4096,512]{1,0:T(8,128)(2,1)} %get-tuple-element.54, bf16[2,256,1024]{2,1,0:T(8,128)(2,1)} %all-gather.12.cloned.1.call-done), kind=kOutput, calls=%fused_computation.34 | convolution fusion | flops 2147483648 | bytes 19398656 | tf_op jit(solution)/shard_map/dot_general | solution.py:83
  165.1 67.0 %all-gather.14.cloned.1.call-done = bf16[4096,1024]{1,0:T(8,128)(2,1)} async-done(((bf16[256,1024]{1,0:T(8,128)(2,1)}), bf16[4096,1024]{1,0:T(8,128)(2,1)}) %all-gather.14.cloned.1.call-update) | async-done | bytes 8388624 | tf_op jit(solution)/shard_map/all_gather | solution.py:138
  232.1 19.3 %fusion.1 = (f32[4096]{0:T(1024)}, f32[4096,1024]{1,0:T(8,128)}) fusion(bf16[4096,1024]{1,0:T(8,128)(2,1)} %all-gather.14.cloned.1.call-done, bf16[2,256,1024]{2,1,0:T(8,128)(2,1)} %all-gather.12.cloned.1.call-done, bf16[4096,512]{1,0:T(8,128)(2,1)} %get-tuple-element.54, f32[4096,1024]{1,0:T(8,128)} %fusion.22), kind=kOutput, calls=%fused_computation.3 | convolution fusion | flops 2176839680 | bytes 44580864 | tf_op jit(solution)/shard_map/dot_general | solution.py:83
  255.5 5.9 all-to-all-done.1
  261.7 9.1 all_to_all.8
  270.8 16.6 %multiply_convert_fusion.1 = (bf16[4096,512]{1,0:T(8,128)(2,1)}, bf16[4096,512]{1,0:T(8,128)(2,1)S(1)}) fusion(f32[4096,512]{1,0:T(8,128)} %copy-done.52, f32[4096,512]{1,0:T(8,128)} %get-tuple-element.55, bf16[512,1024]{1,0:T(8,128)(2,1)} %bitcast.141, bf16[4096,1024]{1,0:T(8,128)(2,1)} %all-gather.14.cloned.1.call-done, f32[4096]{0:T(1024)S(1)} %bitcast.156), kind=kOutput, calls=%fused_computation.7 | convolution fusion | flops 4334813184 | bytes 34619392 | tf_op jit(solution)/shard_map/td,fd->tf/dot_general | solution.py:94
  287.4 8.1 fusion.15
  295.5 8.1 fusion.19
  303.6 8.1 fusion.17
  311.7 20.9 %add_convert_fusion = bf16[4096,1024]{1,0:T(8,128)(2,1)} fusion(f32[4096,1024]{1,0:T(8,128)} %fusion.15, f32[4096,1024]{1,0:T(8,128)} %fusion.19, f32[4096,1024]{1,0:T(8,128)} %fusion.17, bf16[4096,512]{1,0:T(8,128)(2,1)S(1)} %copy-done.12, bf16[2,1024,256]{2,1,0:T(8,128)(2,1)} %all-gather.10.cloned.1.call-done), kind=kOutput, calls=%fused_computation.4 | convolution fusion | flops 2172649472 | bytes 61341696 | tf_op jit(solution)/shard_map/tf,df->td/dot_general | solution.py:109
  332.7 11.0 %multiply_convert_fusion = bf16[4096,1024]{1,0:T(8,128)(2,1)} fusion(f32[4096,1024]{1,0:T(8,128)} %get-tuple-element.57, f32[4096]{0:T(1024)S(1)} %bitcast.157), kind=kLoop, calls=%fused_computation.5 | loop fusion | flops 8388608 | bytes 25182208 | tf_op jit(solution)/shard_map/convert_element_type | solution.py:92
  343.7 11.9 %fusion.7 = f32[512,1024]{1,0:T(8,128)} fusion(bf16[4096,512]{1,0:T(8,128)(2,1)} %get-tuple-element.54, bf16[4096,1024]{1,0:T(8,128)(2,1)} %all-gather.14.cloned.1.call-done, f32[4096]{0:T(1024)S(1)} %bitcast.158), kind=kOutput, calls=%fused_computation.22 | convolution fusion | flops 4307550208 | bytes 14696448 | tf_op jit(solution)/shard_map/tf,td->fd/dot_general | solution.py:99
  355.7 10.4 %fusion.84 = f32[1024,512]{1,0:T(8,128)} fusion(bf16[4096,1024]{1,0:T(8,128)(2,1)} %all-gather.6.cloned.1.call-done, bf16[4096,512]{1,0:T(8,128)(2,1)} %copy-done.10), kind=kOutput, calls=%fused_computation.146 | convolution fusion | flops 4294967296 | bytes 14680064 | tf_op jit(solution)/shard_map/td,tf->df/dot_general | solution.py:100
  367.0 10.6 %fusion.85 = f32[1024,512]{1,0:T(8,128)} fusion(bf16[4096,1024]{1,0:T(8,128)(2,1)} %all-gather.6.cloned.1.call-done, bf16[4096,512]{1,0:T(8,128)(2,1)} %get-tuple-element.30), kind=kOutput, calls=%fused_computation.147 | convolution fusion | flops 4294967296 | bytes 14680064 | tf_op jit(solution)/shard_map/td,tf->df/dot_general | solution.py:101
  377.8 56.9 %reduce-scatter.8.cloned.1.call-done = bf16[256,1024]{1,0:T(8,128)(2,1)} async-done(((bf16[4096,1024]{1,0:T(8,128)(2,1)}), bf16[256,1024]{1,0:T(8,128)(2,1)}) %reduce-scatter.8.cloned.1.call-update) | async-done | bytes 524304 | tf_op jit(solution)/shard_map/reduce_scatter | solution.py:211
  437.2 106.0 %reduce-scatter.6.cloned.1.call-done = bf16[256,1024]{1,0:T(8,128)(2,1)} async-done(((bf16[4096,1024]{1,0:T(8,128)(2,1)}), bf16[256,1024]{1,0:T(8,128)(2,1)}) %reduce-scatter.6.cloned.1.call-update) | async-done | bytes 524304 | tf_op jit(solution)/shard_map/reduce_scatter | solution.py:210
  571.3 40.7 %all-reduce = (f32[1024]{0:T(1024)}, f32[1024]{0:T(1024)}, f32[16]{0:T(128)S(1)}) all-reduce(f32[1024]{0:T(1024)S(1)} %get-tuple-element.15, f32[1024]{0:T(1024)S(1)} %get-tuple-element.13, f32[16]{0:T(128)S(1)} %get-tuple-element.17), channel_id=1, replica_groups=mesh['ep'=16,'hs'=2] {'ep','hs'}, use_global_device_ids=true, to_apply=%region_19.20 | all-reduce | flops 2064 | bytes 16512 | tf_op jit(solution)/shard_map/psum | solution.py:312
  615.4 32.5 %reduce-scatter.12.cloned.1.call-done = f32[1024,256]{1,0:T(8,128)} async-done(((f32[1024,512]{1,0:T(8,128)}), f32[1024,256]{1,0:T(8,128)}) %reduce-scatter.12.cloned.1.call-update) | async-done | bytes 1048592 | tf_op jit(solution)/shard_map/reduce_scatter | solution.py:229
  647.8 245.6 %all-reduce.4.cloned.1.call-done = (f32[1024,1024]{1,0:T(8,128)}, f32[1024,512]{1,0:T(8,128)}, f32[1024,512]{1,0:T(8,128)}, f32[1024,1024]{1,0:T(8,128)}, f32[1024,16]{0,1:T(8,128)}) async-done(((f32[1024,1024]{1,0:T(8,128)}, f32[1024,512]{1,0:T(8,128)}, f32[1024,512]{1,0:T(8,128)}, f32[1024,1024]{1,0:T(8,128)}, f32[1024,16]{0,1:T(8,128)}), (f32[1024,1024]{1,0:T(8,128)}, f32[1024,512]{1,0:T(8,128)}, ...) | async-done | bytes 12648464 | tf_op jit(solution)/shard_map/psum | solution.py:312
  (195 shorter events, 77.9 us)
Async XLA Ops:
  7.2 15.9 %copy-start = (bf16[1024,1024]{1,0:T(8,128)(2,1)S(1)}, bf16[1024,1024]{1,0:T(8,128)(2,1)}, u32[]{:S(2)}) copy-start(bf16[1024,1024]{1,0:T(8,128)(2,1)} %param.23) | copy-start | bytes 6291460
  7.2 26.4 %all-gather.10.cloned.1.call-start = ((), (), s32[]{:S(2)}) async-start(), calls=%async_computation.9 | async-start | bytes 1572864 | tf_op jit(solution)/shard_map/all_gather | solution.py:140
  8.0 48.6 %all-gather.8.cloned.1.call-start = ((), (), s32[]{:S(2)}) async-start(), calls=%async_computation.8 | async-start | bytes 1572864 | tf_op jit(solution)/shard_map/all_gather | solution.py:139
  8.7 125.5 %all-gather.6.cloned.1.call-start = ((), (), s32[]{:S(2)}) async-start(), calls=%async_computation.7 | async-start | bytes 8912896 | tf_op jit(solution)/shard_map/all_gather | solution.py:199
  25.9 129.3 %all-gather.12.cloned.1.call-start = ((), (), s32[]{:S(2)}) async-start(), calls=%async_computation.10 | async-start | bytes 1572864 | tf_op jit(solution)/shard_map/all_gather | solution.py:141
  26.4 205.7 %all-gather.14.cloned.1.call-start = ((), (), s32[]{:S(2)}) async-start(), calls=%async_computation.12 | async-start | bytes 8912896 | tf_op jit(solution)/shard_map/all_gather | solution.py:138
  134.2 11.2 %copy-start.51 = (bf16[4096,1024]{1,0:T(8,128)(2,1)S(1)}, bf16[4096,1024]{1,0:T(8,128)(2,1)}, u32[]{:S(2)}) copy-start(bf16[4096,1024]{1,0:T(8,128)(2,1)} %all-gather.6.cloned.1.call-done) | copy-start | bytes 25165828
  165.1 90.1 %copy-start.9 = (bf16[256,1024]{1,0:T(8,128)(2,1)S(1)}, bf16[256,1024]{1,0:T(8,128)(2,1)}, u32[]{:S(2)}) copy-start(bf16[256,1024]{1,0:T(8,128)(2,1)} %multiply_convert_fusion.4) | copy-start | bytes 1572868
  165.1 90.1 %copy-start.41 = (bf16[1024,16]{0,1:T(8,128)(2,1)S(1)}, bf16[1024,16]{0,1:T(8,128)(2,1)}, u32[]{:S(2)}) copy-start(bf16[1024,16]{0,1:T(8,128)(2,1)} %param.25) | copy-start | bytes 98308
  165.1 90.3 %copy-start.50 = (s32[1,256]{1,0:T(1,128)S(1)}, s32[1,256]{1,0:T(1,128)}, u32[]{:S(2)}) copy-start(s32[1,256]{1,0:T(1,128)} %param.17) | copy-start | bytes 3076
  165.1 96.3 %copy-start.47 = (s32[256,8]{0,1:T(8,128)S(1)}, s32[256,8]{0,1:T(8,128)}, u32[]{:S(2)}) copy-start(s32[256,8]{0,1:T(8,128)} %param.18) | copy-start | bytes 24580
  251.4 10.0 %all-to-all-start.1 = ((f32[16,1,256]{2,1,0:T(1,128)}), f32[16,1,256]{2,1,0:T(1,128)S(1)}, u32[]{:S(2)}, u32[]{:S(2)}) async-start(f32[16,1,256]{2,1,0:T(1,128)} %bitcast.24), calls=%async_computation.3 | async-start | bytes 32768 | tf_op jit(solution)/shard_map/all_to_all | solution.py:217
  254.9 179.8 %reduce-scatter.8.cloned.1.call-start = ((), (), s32[]{:S(2)}) async-start(), calls=%async_computation.13 | async-start | bytes 8912896 | tf_op jit(solution)/shard_map/reduce_scatter | solution.py:211
  270.8 16.6 %copy-start.16 = (bf16[2,1024,256]{2,1,0:T(8,128)(2,1)S(1)}, bf16[2,1024,256]{2,1,0:T(8,128)(2,1)}, u32[]{:S(2)}) copy-start(bf16[2,1024,256]{2,1,0:T(8,128)(2,1)} %all-gather.8.cloned.1.call-done) | copy-start | bytes 3145732
  295.5 8.1 copy-start.11
  295.5 8.1 copy-start.15
  332.6 210.6 %reduce-scatter.6.cloned.1.call-start = ((), (), s32[]{:S(2)}) async-start(), calls=%async_computation.11 | async-start | bytes 8912896 | tf_op jit(solution)/shard_map/reduce_scatter | solution.py:210
  343.7 271.7 %reduce-scatter.14.cloned.1.call-start = ((), (), s32[]{:S(2)}) async-start(), calls=%async_computation.16 | async-start | bytes 3145728 | tf_op jit(solution)/shard_map/reduce_scatter | solution.py:230
  355.6 259.7 %reduce-scatter.10.cloned.1.call-start = ((), (), s32[]{:S(2)}) async-start(), calls=%async_computation.14 | async-start | bytes 3145728 | tf_op jit(solution)/shard_map/reduce_scatter | solution.py:228
  366.1 281.7 %reduce-scatter.12.cloned.1.call-start = ((), (), s32[]{:S(2)}) async-start(), calls=%async_computation.15 | async-start | bytes 3145728 | tf_op jit(solution)/shard_map/reduce_scatter | solution.py:229
  367.0 67.7 %copy-start.6 = (f32[256,1024]{1,0:T(8,128)S(1)}, f32[256,1024]{1,0:T(8,128)}, u32[]{:S(2)}) copy-start(f32[256,1024]{1,0:T(8,128)} %copy-done.5) | copy-start | bytes 3145732
  367.0 67.7 %copy-start.46 = (f32[1024]{0:T(1024)S(1)}, f32[1024]{0:T(1024)}, u32[]{:S(2)}) copy-start(f32[1024]{0:T(1024)} %param.24) | copy-start | bytes 12292
  367.0 67.7 %copy-start.49 = (f32[256]{0:T(256)S(1)}, f32[256]{0:T(256)}, u32[]{:S(2)}) copy-start(f32[256]{0:T(256)} %copy-done.48) | copy-start | bytes 3076
  377.6 515.9 %all-reduce.4.cloned.1.call-start = ((), (), s32[]{:S(2)}) async-start(), calls=%async_computation.17 | async-start | bytes 25296896 | tf_op jit(solution)/shard_map/psum | solution.py:312
  (41 other events, 129.3 us)
Sparse Core Ops, SparseCore 0:
  9.6 23.9 all-gather.9
  35.2 21.2 all-gather.7
  59.3 74.8 all-gather.5
  135.6 19.5 all-gather.11
  157.2 74.8 all-gather.13
  332.7 101.9 reduce-scatter.7
  438.8 104.4 reduce-scatter.5
  546.1 31.5 reduce-scatter.13
  580.6 32.6 reduce-scatter.9
  616.0 31.8 reduce-scatter.11
  656.5 236.8 all-reduce.3
where the time goes:
time: 917 us; the launch traced here: 911 us
  waiting for transfers between devices  621 us (68%)
  matrix products  174 us (19%)
  blocking collectives  49.7 us (5%)
  other arithmetic  24.5 us (3%)
  local copies, waits for them, and re-layouts  22.9 us (2%)
  between operations  14.7 us (2%)
    psum x1, waiting for transfers between devices, local(): lax.psum((attn_gain_grad, query_w_grad, key_w_grad, value_w_grad, out_w_g...  246 us
    reduce_scatter x1, waiting for transfers between devices, local(): lax.psum_scatter(weighted, 'ep', scatter_dimension=0, tiled=True)  106 us
    all_gather x1, waiting for transfers between devices, local(): rows_all = lax.all_gather(moe_in, 'ep', axis=0, tiled=True)  75.4 us
    all_gather x1, waiting for transfers between devices, local(): upstream_all = lax.all_gather(cotangent, 'ep', axis=0, tiled=True)  67 us
    reduce_scatter x1, waiting for transfers between devices, local(): lax.psum_scatter(back, 'ep', scatter_dimension=0, tiled=True)  56.9 us
    psum x1, blocking collectives, local(): lax.psum((attn_gain_grad, query_w_grad, key_w_grad, value_w_grad, out_w_g...  40.7 us
    reduce_scatter x1, waiting for transfers between devices, local(): lax.psum_scatter(up_w_grad, 'hs', scatter_dimension=1, tiled=True)[None]  32.5 us
    dot_general x2, matrix products, expert_pass(): jnp.dot(hidden[:, j * width:(j + 1) * width], down_w[j], preferred_elemen...  29.2 us
  transfers between devices with their start and end apart: 12, of which 10 were waited for; matrix products, arithmetic and copies ran while one was open for 13% of the time, Pallas kernels for 0%

commit v1 on v0

--- a/solution.py
+++ b/solution.py
@@ -310,17 +310,20 @@
     input_norm_grad, attn_gain_grad = rms_backward(inputs, inverse_one, attn_gain, normed_grad)
     input_grad = middle_grad + input_norm_grad
     shared = lax.psum(
-        (
-            attn_gain_grad,
-            query_w_grad,
-            key_w_grad,
-            value_w_grad,
-            out_w_grad,
-            moe_gain_grad,
-            router_w_grad,
-            counts_local,
+        lax.psum(
+            (
+                attn_gain_grad,
+                query_w_grad,
+                key_w_grad,
+                value_w_grad,
+                out_w_grad,
+                moe_gain_grad,
+                router_w_grad,
+                counts_local,
+            ),
+            "hs",
         ),
-        ("ep", "hs"),
+        "ep",
     )
     return (
         output,

time: 917 us -> 1230 us (1.34)
  waiting for transfers between devices: 621 us -> 934 us
    psum x0 -> x1, waiting for transfers between devices: none -> 244 us  [local(): lax.psum(lax.psum((attn_gain_grad, query_w_grad, key_w_grad, value_w_grad...]
    psum x1, blocking collectives: 40.7 us -> 5.04 us  [local(): lax.psum((attn_gain_grad, query_w_grad, key_w_grad, value_w_grad, out_w_g...]
    psum x0 -> x1, blocking collectives: none -> 33.6 us  [local(): lax.psum(lax.psum((attn_gain_grad, query_w_grad, key_w_grad, value_w_grad...]
    reduce_scatter x1, waiting for transfers between devices: 56.9 us -> 90.1 us  [local(): lax.psum_scatter(back, 'ep', scatter_dimension=0, tiled=True)]
    reduce_scatter x1, waiting for transfers between devices: 0.01 us -> 22.3 us  [local(): lax.psum_scatter(gate_w_grad, 'hs', scatter_dimension=1, tiled=True)[None]]
    psum x1, waiting for transfers between devices: 246 us -> 259 us  [local(): lax.psum((attn_gain_grad, query_w_grad, key_w_grad, value_w_grad, out_w_g...]
  transfers between devices with their start and end apart: 12 -> 13, of which waited for: 10 -> 12; matrix products, arithmetic and copies ran while one was open for 13% -> 8% of each run, Pallas kernels for 0% -> 0%
where the time goes in v1:
time: 1230 us
  waiting for transfers between devices  934 us (76%)
  matrix products  175 us (14%)
  blocking collectives  47.7 us (4%)
  other arithmetic  25.2 us (2%)
  local copies, waits for them, and re-layouts  25.1 us (2%)
  between operations  15 us (1%)
    psum x1, waiting for transfers between devices, local(): lax.psum((attn_gain_grad, query_w_grad, key_w_grad, value_w_grad, out_w_g...  259 us
    psum x1, waiting for transfers between devices, local(): lax.psum(lax.psum((attn_gain_grad, query_w_grad, key_w_grad, value_w_grad...  244 us
    reduce_scatter x1, waiting for transfers between devices, local(): lax.psum_scatter(weighted, 'ep', scatter_dimension=0, tiled=True)  105 us
    reduce_scatter x1, waiting for transfers between devices, local(): lax.psum_scatter(back, 'ep', scatter_dimension=0, tiled=True)  90.1 us
    all_gather x1, waiting for transfers between devices, local(): rows_all = lax.all_gather(moe_in, 'ep', axis=0, tiled=True)  75.4 us
    all_gather x1, waiting for transfers between devices, local(): upstream_all = lax.all_gather(cotangent, 'ep', axis=0, tiled=True)  67 us
    reduce_scatter x1, waiting for transfers between devices, local(): lax.psum_scatter(up_w_grad, 'hs', scatter_dimension=1, tiled=True)[None]  34.7 us
    psum x1, blocking collectives, local(): lax.psum(lax.psum((attn_gain_grad, query_w_grad, key_w_grad, value_w_grad...  33.6 us
  transfers between devices with their start and end apart: 13, of which 12 were waited for; matrix products, arithmetic and copies ran while one was open for 8% of the time, Pallas kernels for 0%

profile of v1, /device:TPU:0, one launch (start us, length us, event | category | flops | bytes accessed | tf_op | source)
XLA Modules:
  0.0 1227.1 jit_solution(4702721604026191408)
XLA Ops:
  35.7 20.8 %all-gather.8.cloned.1.call-done = bf16[2,1024,256]{2,1,0:T(8,128)(2,1)} async-done(((bf16[1,1024,256]{2,1,0:T(8,128)(2,1)}), bf16[2,1024,256]{2,1,0:T(8,128)(2,1)}) %all-gather.8.cloned.1.call-update) | async-done | bytes 1048592 | tf_op jit(solution)/shard_map/all_gather | solution.py:139
  58.8 75.4 %all-gather.6.cloned.1.call-done = bf16[4096,1024]{1,0:T(8,128)(2,1)} async-done(((bf16[256,1024]{1,0:T(8,128)(2,1)}), bf16[4096,1024]{1,0:T(8,128)(2,1)}) %all-gather.6.cloned.1.call-update) | async-done | bytes 8388624 | tf_op jit(solution)/shard_map/all_gather | solution.py:199
  134.2 7.4 fusion.46
  144.9 8.8 multiply_convert_fusion.3
  155.2 9.9 fusion.22
  165.1 67.0 %all-gather.14.cloned.1.call-done = bf16[4096,1024]{1,0:T(8,128)(2,1)} async-done(((bf16[256,1024]{1,0:T(8,128)(2,1)}), bf16[4096,1024]{1,0:T(8,128)(2,1)}) %all-gather.14.cloned.1.call-update) | async-done | bytes 8388624 | tf_op jit(solution)/shard_map/all_gather | solution.py:138
  232.1 19.3 %fusion.1 = (f32[4096]{0:T(1024)}, f32[4096,1024]{1,0:T(8,128)}) fusion(bf16[4096,1024]{1,0:T(8,128)(2,1)} %all-gather.14.cloned.1.call-done, bf16[2,256,1024]{2,1,0:T(8,128)(2,1)} %all-gather.12.cloned.1.call-done, bf16[4096,512]{1,0:T(8,128)(2,1)} %get-tuple-element.62, f32[4096,1024]{1,0:T(8,128)} %fusion.22), kind=kOutput, calls=%fused_computation.3 | convolution fusion | flops 2176839680 | bytes 44580864 | tf_op jit(solution)/shard_map/dot_general | solution.py:83
  262.2 9.1 all_to_all.8
  271.3 16.6 %multiply_convert_fusion.1 = (bf16[4096,512]{1,0:T(8,128)(2,1)}, bf16[4096,512]{1,0:T(8,128)(2,1)S(1)}) fusion(f32[4096,512]{1,0:T(8,128)} %copy-done.47, f32[4096,512]{1,0:T(8,128)} %get-tuple-element.63, bf16[512,1024]{1,0:T(8,128)(2,1)} %bitcast.141, bf16[4096,1024]{1,0:T(8,128)(2,1)} %all-gather.14.cloned.1.call-done, f32[4096]{0:T(1024)S(1)} %bitcast.156), kind=kOutput, calls=%fused_computation.7 | convolution fusion | flops 4334813184 | bytes 34619392 | tf_op jit(solution)/shard_map/td,fd->tf/dot_general | solution.py:94
  287.9 8.1 fusion.15
  296.0 8.1 fusion.19
  304.1 8.1 fusion.17
  312.2 20.9 %add_convert_fusion = bf16[4096,1024]{1,0:T(8,128)(2,1)} fusion(f32[4096,1024]{1,0:T(8,128)} %fusion.15, f32[4096,1024]{1,0:T(8,128)} %fusion.19, f32[4096,1024]{1,0:T(8,128)} %fusion.17, bf16[4096,512]{1,0:T(8,128)(2,1)S(1)} %copy-done.10, bf16[2,1024,256]{2,1,0:T(8,128)(2,1)} %all-gather.10.cloned.1.call-done), kind=kOutput, calls=%fused_computation.4 | convolution fusion | flops 2172649472 | bytes 61341696 | tf_op jit(solution)/shard_map/tf,df->td/dot_general | solution.py:109
  333.2 11.0 multiply_convert_fusion
  345.1 90.1 %reduce-scatter.8.cloned.1.call-done = bf16[256,1024]{1,0:T(8,128)(2,1)} async-done(((bf16[4096,1024]{1,0:T(8,128)(2,1)}), bf16[256,1024]{1,0:T(8,128)(2,1)}) %reduce-scatter.8.cloned.1.call-update) | async-done | bytes 524304 | tf_op jit(solution)/shard_map/reduce_scatter | solution.py:211
  438.6 105.1 %reduce-scatter.6.cloned.1.call-done = bf16[256,1024]{1,0:T(8,128)(2,1)} async-done(((bf16[4096,1024]{1,0:T(8,128)(2,1)}), bf16[256,1024]{1,0:T(8,128)(2,1)}) %reduce-scatter.6.cloned.1.call-update) | async-done | bytes 524304 | tf_op jit(solution)/shard_map/reduce_scatter | solution.py:210
  568.7 10.7 fusion.7
  579.5 10.4 fusion.84
  590.0 10.6 fusion.85
  600.9 259.3 %all-reduce.9.cloned.1.call-done = (f32[1024,1024]{1,0:T(8,128)}, f32[1024,512]{1,0:T(8,128)}, f32[1024,512]{1,0:T(8,128)}, f32[1024,1024]{1,0:T(8,128)}, f32[1024,16]{0,1:T(8,128)}) async-done(((f32[1024,1024]{1,0:T(8,128)}, f32[1024,512]{1,0:T(8,128)}, f32[1024,512]{1,0:T(8,128)}, f32[1024,1024]{1,0:T(8,128)}, f32[1024,16]{0,1:T(8,128)}), (f32[1024,1024]{1,0:T(8,128)}, f32[1024,512]{1,0:T(8,128)}, ...) | async-done | bytes 12648464 | tf_op jit(solution)/shard_map/psum | solution.py:313
  870.9 33.6 %all-reduce = (f32[1024]{0:T(1024)}, f32[1024]{0:T(1024)}, f32[16]{0:T(128)S(1)}) all-reduce(f32[1024]{0:T(1024)S(1)} %get-tuple-element.30, f32[1024]{0:T(1024)S(1)} %get-tuple-element.31, f32[16]{0:T(128)S(1)} %get-tuple-element.32), channel_id=1, replica_groups=mesh['ep'=16,'hs'=2] {'ep'}, use_global_device_ids=true, to_apply=%region_20.21 | all-reduce | flops 2064 | bytes 16512 | tf_op jit(solution)/shard_map/psum | solution.py:312
  907.8 22.3 %reduce-scatter.10.cloned.1.call-done = f32[1024,256]{1,0:T(8,128)} async-done(((f32[1024,512]{1,0:T(8,128)}), f32[1024,256]{1,0:T(8,128)}) %reduce-scatter.10.cloned.1.call-update) | async-done | bytes 1048592 | tf_op jit(solution)/shard_map/reduce_scatter | solution.py:228
  930.0 34.7 %reduce-scatter.12.cloned.1.call-done = f32[1024,256]{1,0:T(8,128)} async-done(((f32[1024,512]{1,0:T(8,128)}), f32[1024,256]{1,0:T(8,128)}) %reduce-scatter.12.cloned.1.call-update) | async-done | bytes 1048592 | tf_op jit(solution)/shard_map/reduce_scatter | solution.py:229
  964.7 244.0 %all-reduce.7.cloned.1.call-done = (f32[1024,1024]{1,0:T(8,128)}, f32[1024,512]{1,0:T(8,128)}, f32[1024,512]{1,0:T(8,128)}, f32[1024,1024]{1,0:T(8,128)}, f32[1024,16]{0,1:T(8,128)}) async-done(((f32[1024,1024]{1,0:T(8,128)}, f32[1024,512]{1,0:T(8,128)}, f32[1024,512]{1,0:T(8,128)}, f32[1024,1024]{1,0:T(8,128)}, f32[1024,16]{0,1:T(8,128)}), (f32[1024,1024]{1,0:T(8,128)}, f32[1024,512]{1,0:T(8,128)}, ...) | async-done | bytes 12648464 | tf_op jit(solution)/shard_map/psum | solution.py:312
  (189 shorter events, 100.7 us)
Async XLA Ops:
  7.2 16.7 %copy-start = (bf16[1024,1024]{1,0:T(8,128)(2,1)S(1)}, bf16[1024,1024]{1,0:T(8,128)(2,1)}, u32[]{:S(2)}) copy-start(bf16[1024,1024]{1,0:T(8,128)(2,1)} %param.23) | copy-start | bytes 6291460
  7.2 26.4 %all-gather.10.cloned.1.call-start = ((), (), s32[]{:S(2)}) async-start(), calls=%async_computation.9 | async-start | bytes 1572864 | tf_op jit(solution)/shard_map/all_gather | solution.py:140
  8.0 48.6 %all-gather.8.cloned.1.call-start = ((), (), s32[]{:S(2)}) async-start(), calls=%async_computation.8 | async-start | bytes 1572864 | tf_op jit(solution)/shard_map/all_gather | solution.py:139
  8.7 125.5 %all-gather.6.cloned.1.call-start = ((), (), s32[]{:S(2)}) async-start(), calls=%async_computation.7 | async-start | bytes 8912896 | tf_op jit(solution)/shard_map/all_gather | solution.py:199
  26.6 128.6 %all-gather.12.cloned.1.call-start = ((), (), s32[]{:S(2)}) async-start(), calls=%async_computation.10 | async-start | bytes 1572864 | tf_op jit(solution)/shard_map/all_gather | solution.py:141
  27.2 204.9 %all-gather.14.cloned.1.call-start = ((), (), s32[]{:S(2)}) async-start(), calls=%async_computation.12 | async-start | bytes 8912896 | tf_op jit(solution)/shard_map/all_gather | solution.py:138
  134.2 10.7 copy-start.30
  134.2 10.7 copy-start.46
  165.1 90.1 %copy-start.7 = (bf16[256,1024]{1,0:T(8,128)(2,1)S(1)}, bf16[256,1024]{1,0:T(8,128)(2,1)}, u32[]{:S(2)}) copy-start(bf16[256,1024]{1,0:T(8,128)(2,1)} %multiply_convert_fusion.4) | copy-start | bytes 1572868
  165.1 90.1 %copy-start.35 = (bf16[1024,16]{0,1:T(8,128)(2,1)S(1)}, bf16[1024,16]{0,1:T(8,128)(2,1)}, u32[]{:S(2)}) copy-start(bf16[1024,16]{0,1:T(8,128)(2,1)} %param.25) | copy-start | bytes 98308
  165.1 90.4 %copy-start.45 = (s32[1,256]{1,0:T(1,128)S(1)}, s32[1,256]{1,0:T(1,128)}, u32[]{:S(2)}) copy-start(s32[1,256]{1,0:T(1,128)} %param.17) | copy-start | bytes 3076
  165.1 96.3 %copy-start.42 = (s32[256,8]{0,1:T(8,128)S(1)}, s32[256,8]{0,1:T(8,128)}, u32[]{:S(2)}) copy-start(s32[256,8]{0,1:T(8,128)} %param.18) | copy-start | bytes 24580
  251.4 10.0 all-to-all-start.1
  254.9 180.3 %reduce-scatter.8.cloned.1.call-start = ((), (), s32[]{:S(2)}) async-start(), calls=%async_computation.13 | async-start | bytes 8912896 | tf_op jit(solution)/shard_map/reduce_scatter | solution.py:211
  271.3 61.9 %copy-start.37 = (f32[16,1,256]{2,1,0:T(1,128)}, f32[16,1,256]{2,1,0:T(1,128)S(1)}, u32[]{:S(2)}) copy-start(f32[16,1,256]{2,1,0:T(1,128)S(1)} %all_to_all.8) | copy-start | bytes 49156
  271.3 16.6 %copy-start.12 = (bf16[2,1024,256]{2,1,0:T(8,128)(2,1)S(1)}, bf16[2,1024,256]{2,1,0:T(8,128)(2,1)}, u32[]{:S(2)}) copy-start(bf16[2,1024,256]{2,1,0:T(8,128)(2,1)} %all-gather.8.cloned.1.call-done) | copy-start | bytes 3145732
  296.0 8.1 copy-start.9
  296.0 8.1 copy-start.11
  333.1 210.6 %reduce-scatter.6.cloned.1.call-start = ((), (), s32[]{:S(2)}) async-start(), calls=%async_computation.11 | async-start | bytes 8912896 | tf_op jit(solution)/shard_map/reduce_scatter | solution.py:210
  344.2 516.0 %all-reduce.9.cloned.1.call-start = ((), (), s32[]{:S(2)}) async-start(), calls=%async_computation.18 | async-start | bytes 25296896 | tf_op jit(solution)/shard_map/psum | solution.py:313
  568.0 339.7 %reduce-scatter.14.cloned.1.call-start = ((), (), s32[]{:S(2)}) async-start(), calls=%async_computation.16 | async-start | bytes 3145728 | tf_op jit(solution)/shard_map/reduce_scatter | solution.py:230
  579.5 350.6 %reduce-scatter.10.cloned.1.call-start = ((), (), s32[]{:S(2)}) async-start(), calls=%async_computation.14 | async-start | bytes 3145728 | tf_op jit(solution)/shard_map/reduce_scatter | solution.py:228
  590.0 374.8 %reduce-scatter.12.cloned.1.call-start = ((), (), s32[]{:S(2)}) async-start(), calls=%async_computation.15 | async-start | bytes 3145728 | tf_op jit(solution)/shard_map/reduce_scatter | solution.py:229
  600.6 608.1 %all-reduce.7.cloned.1.call-start = ((), (), s32[]{:S(2)}) async-start(), calls=%async_computation.17 | async-start | bytes 25296896 | tf_op jit(solution)/shard_map/psum | solution.py:312
  (37 other events, 122.2 us)
Sparse Core Ops, SparseCore 0:
  9.6 23.9 all-gather.9
  35.2 21.2 all-gather.7
  59.3 74.8 all-gather.5
  135.6 19.5 all-gather.11
  157.2 74.8 all-gather.13
  333.3 101.9 reduce-scatter.7
  439.3 104.4 reduce-scatter.5
  568.2 291.9 all-reduce.8
  863.0 31.8 reduce-scatter.13
  898.2 31.8 reduce-scatter.9
  932.9 31.8 reduce-scatter.11
  970.4 238.2 all-reduce.6
